TPU v7x, 512 devices: a whole 4x8x8 slice. The times are simulated.
512 devices in a mesh: prow: 16 (over y, core), pcol: 32 (over z, x).
Axes of the slice: x: 4, y: 8, z: 8, core: 2. Of those that a mesh axis runs over, the one named last changes fastest.
Arguments:
- embeddings: bfloat16 [12, 16, 128, 768], P(None, 'prow', None, 'pcol'), may hold values from -6 to 6
- noise_var: bfloat16 [12, 16, 128], P(None, 'prow'), may hold values from 0.5 to 2
Outputs:
- schur_block: float32 [12, 16, 128, 6, 32, 128], P(None, 'prow', None, None, 'pcol')
- panel_cols: float32 [12, 16, 128, 128], P(None, 'prow', 'pcol')
All inputs are finite; a program needn't handle non-finite values.
Results may differ from a plain program's by a relative error of at most 0.0003.
Values may be sent and summed in bfloat16 or wider, within the bound.
A program may use at most 64 MiB of HBM per device.

v0:
```python
import jax
import jax.numpy as jnp
from jax import lax
from jax.sharding import PartitionSpec as P


def from_root(value, axis, source):
    kept = jnp.where(lax.axis_index(axis) == source, value, 0).astype(value.dtype)
    return lax.psum(kept, axis)


def squares(values):
    return jnp.sum(jnp.square(values.astype(jnp.float32)), axis=-1)


def kernel_block(left_x, right_x, left_sq, right_sq, feat_width):
    inner_dots = lax.dot_general(
        left_x, right_x, (((1,), (1,)), ((), ())), preferred_element_type=jnp.float32
    )
    return jnp.exp(-(left_sq[:, None] + right_sq[None, :] - 2.0 * inner_dots) / feat_width)


def shards(embeddings, noise_var):
    row_count = lax.axis_size("prow")
    col_count = lax.axis_size("pcol")
    row_index = lax.axis_index("prow")
    col_index = lax.axis_index("pcol")
    features = lax.all_gather(embeddings, "pcol", axis=3, tiled=True)
    row_tiles = features.shape[0]
    tile_size = features.shape[2]
    feat_width = features.shape[3]
    col_tiles = row_tiles * row_count // col_count
    group_ratio = col_count // row_count
    row_x = features.reshape(row_tiles * tile_size, feat_width)
    row_var = noise_var.reshape(row_tiles * tile_size).astype(jnp.float32)
    first_x, first_noise = (
        from_root(features[0, 0], "prow", 0),
        from_root(noise_var[0, 0], "prow", 0),
    )
    first_var = first_noise.astype(jnp.float32)
    grouped = features.reshape(col_tiles, group_ratio, tile_size, feat_width)
    chosen = lax.dynamic_index_in_dim(grouped, col_index // row_count, 1, keepdims=False)
    root_row = col_index % row_count
    col_x = from_root(chosen, "prow", root_row).reshape(col_tiles * tile_size, feat_width)
    row_sq = squares(row_x)
    col_sq = squares(col_x)
    first_sq = squares(first_x)
    offsets = jnp.arange(tile_size, dtype=jnp.int32)
    row_global = (
        (jnp.arange(row_tiles, dtype=jnp.int32) * row_count + row_index)[:, None] * tile_size
        + offsets[None, :]
    ).reshape(-1)
    col_global = (
        (jnp.arange(col_tiles, dtype=jnp.int32) * col_count + col_index)[:, None] * tile_size
        + offsets[None, :]
    ).reshape(-1)
    kernel_local = kernel_block(row_x, col_x, row_sq, col_sq, feat_width)
    kernel_local = kernel_local + jnp.where(
        row_global[:, None] == col_global[None, :], row_var[:, None], jnp.float32(0.0)
    )
    first_kernel = kernel_block(first_x, first_x, first_sq, first_sq, feat_width)
    first_kernel = first_kernel + jnp.where(
        offsets[:, None] == offsets[None, :], first_var[None, :], jnp.float32(0.0)
    )
    factor = jnp.linalg.cholesky(first_kernel)
    candidate = lax.linalg.triangular_solve(
        factor, kernel_local[:, :tile_size], left_side=False, lower=True, transpose_a=True
    )
    row_panel = from_root(candidate, "pcol", 0)
    regrouped = row_panel.reshape(col_tiles, group_ratio, tile_size, tile_size)
    picked = lax.dynamic_index_in_dim(regrouped, col_index // row_count, 1, keepdims=False)
    col_panel = from_root(picked, "prow", root_row).reshape(col_tiles * tile_size, tile_size)
    update = lax.dot_general(
        row_panel,
        col_panel,
        (((1,), (1,)), ((), ())),
        precision=lax.Precision.HIGHEST,
        preferred_element_type=jnp.float32,
    )
    schur_block = (kernel_local - update).reshape(row_tiles, 1, tile_size, col_tiles, 1, tile_size)
    share = tile_size // col_count
    panel_cols = lax.dynamic_slice_in_dim(
        row_panel.reshape(row_tiles, 1, tile_size, tile_size), col_index * share, share, 2
    )
    return (schur_block, panel_cols)


def solution(mesh):
    placed = (P(None, "prow", None, "pcol"), P(None, "prow", None))
    return jax.shard_map(
        shards,
        mesh=mesh,
        in_specs=placed,
        out_specs=(P(None, "prow", None, None, "pcol", None), P(None, "prow", "pcol", None)),
        check_vma=False,
    )
```

profile of v0, /device:TPU:1, one launch (start us, length us, event | category | flops | bytes accessed | tf_op | source)
XLA Modules:
  0.0 566.9 jit_solution(10739975928645798636)
XLA Ops:
  7.2 0.7 all-gather.2.cloned.1.call-update
  8.0 0.7 fusion.9
  8.7 29.8 %psum.37 = bf16[128]{0:T(256)(128)(2,1)S(1)} all-reduce(bf16[128]{0:T(256)(128)(2,1)S(1)} %fusion.9), channel_id=1, replica_groups=mesh['prow'=16,'pcol'=32] {'prow'}, use_global_device_ids=true, to_apply=%region_5.6 | all-reduce | flops 128 | bytes 512 | tf_op jit(solution)/shard_map/psum | solution.py:9
  38.6 57.0 %all-gather.2.cloned.1.call-done = bf16[12,1,128,768]{2,3,1,0:T(8,128)(2,1)} async-done(((bf16[12,1,128,24]{2,3,1,0:T(8,128)(2,1)}), bf16[12,1,128,768]{2,3,1,0:T(8,128)(2,1)}) %all-gather.2.cloned.1.call-update) | async-done | bytes 2359312 | tf_op jit(solution)/shard_map/all_gather | solution.py:28
  95.6 4.4 copy.23
  100.0 2.4 select_bitcast_fusion
  102.4 0.7 fusion.5
  103.7 119.9 %all-reduce.9.cloned.1.call-done = (bf16[6,128,768]{2,1,0:T(8,128)(2,1)}, bf16[128,768]{0,1:T(8,128)(2,1)}) async-done(((bf16[6,128,768]{2,1,0:T(8,128)(2,1)}, bf16[128,768]{0,1:T(8,128)(2,1)}), (bf16[6,128,768]{2,1,0:T(8,128)(2,1)}, bf16[128,768]{0,1:T(8,128)(2,1)})) %all-reduce.9.cloned.1.call-update) | async-done | bytes 1376272 | tf_op jit(solution)/shard_map/psum | solution.py:9
  223.6 1.0 multiply_reduce_fusion.2
  224.6 1.3 broadcast_add_fusion
  226.0 1.6 multiply_reduce_fusion.1
  227.8 11.7 %cholesky.16 = f32[128,128]{1,0:T(8,128)S(1)} custom-call(f32[128,128]{1,0:T(8,128)S(1)} %add_multiply_fusion), custom_call_target="Cholesky" | custom-call | tf_op jit(solution)/shard_map/jit(cholesky)/cholesky | solution.py:65
  240.2 0.7 fusion.6
  240.8 9.8 %custom-call.6 = f32[1,128,128]{1,2,0:T(8,128)S(1)} custom-call(f32[1,128,128]{2,1,0:T(8,128)S(1)} %fusion.6), custom_call_target="InvertDiagBlocksLowerTriangular" | custom-call | tf_op jit(solution)/shard_map/triangular_solve | solution.py:66
  250.6 4.6 fusion.3
  255.3 2.2 copy-done.1
  257.4 2.3 convolution_select_fusion
  260.0 156.8 %all-reduce.5.cloned.1.call-done = f32[1536,128]{1,0:T(8,128)} async-done(((f32[1536,128]{1,0:T(8,128)}), f32[1536,128]{1,0:T(8,128)}) %all-reduce.5.cloned.1.call-update) | async-done | bytes 786448 | tf_op jit(solution)/shard_map/psum | solution.py:9
  416.8 1.8 dynamic-slice_select_fusion
  418.6 1.4 constant_dynamic-slice_fusion
  420.0 115.0 %all-reduce.7.cloned.1.call-done = f32[768,128]{1,0:T(8,128)} async-done(((f32[768,128]{1,0:T(8,128)}), f32[768,128]{1,0:T(8,128)}) %all-reduce.7.cloned.1.call-update) | async-done | bytes 393232 | tf_op jit(solution)/shard_map/psum | solution.py:9
  535.0 8.7 %convolution_subtract_fusion = f32[1536,768]{0,1:T(8,128)} fusion(f32[1536,768]{0,1:T(8,128)} %copy-done.1, f32[1536,128]{1,0:T(8,128)} %all-reduce.5.cloned.1.call-done, f32[768,128]{1,0:T(8,128)} %all-reduce.7.cloned.1.call-done), kind=kOutput, calls=%fused_computation.6 | convolution fusion | flops 1813118976 | bytes 10616832 | tf_op jit(solution)/shard_map/dot_general | solution.py:73
  543.8 6.7 %reshape.116 = f32[12,1,128,6,1,128]{2,0,5,3,4,1:T(8,128)} reshape(f32[1536,768]{0,1:T(8,128)} %convolution_subtract_fusion) | data formatting | bytes 9437184 | tf_op jit(solution)/shard_map/reshape | solution.py:80
  550.4 9.9 %copy.30 = f32[12,1,128,6,1,128]{5,4,3,2,1,0:T(1,128)} copy(f32[12,1,128,6,1,128]{2,0,5,3,4,1:T(8,128)} %reshape.116) | data formatting | bytes 9437184
  (24 shorter events, 2.0 us)
Async XLA Ops:
  7.2 96.1 %copy-start.2 = (bf16[12,1,128]{2,0,1:T(8,128)(2,1)S(1)}, bf16[12,1,128]{2,0,1:T(8,128)(2,1)}, u32[]{:S(2)}) copy-start(bf16[12,1,128]{2,0,1:T(8,128)(2,1)} %param.3) | copy-start | bytes 9220
  7.2 88.4 %all-gather.2.cloned.1.call-start = ((), (), s32[]{:S(2)}) async-start(), calls=%async_computation | async-start | bytes 2433024 | tf_op jit(solution)/shard_map/all_gather | solution.py:28
  7.9 215.7 %all-reduce.9.cloned.1.call-start = ((), (), s32[]{:S(2)}) async-start(), calls=%async_computation.3 | async-start | bytes 2752512 | tf_op jit(solution)/shard_map/psum | solution.py:9
  95.6 6.8 %copy-start = (bf16[12,1,128,768]{2,3,1,0:T(8,128)(2,1)S(1)}, bf16[12,1,128,768]{2,3,1,0:T(8,128)(2,1)}, u32[]{:S(2)}) copy-start(bf16[12,1,128,768]{2,3,1,0:T(8,128)(2,1)} %all-gather.2.cloned.1.call-done) | copy-start | bytes 7077892
  103.1 313.7 %all-reduce.5.cloned.1.call-start = ((), (), s32[]{:S(2)}) async-start(), calls=%async_computation.1 | async-start | bytes 1572864 | tf_op jit(solution)/shard_map/psum | solution.py:9
  255.3 2.2 copy-start.1
  259.8 275.2 %all-reduce.7.cloned.1.call-start = ((), (), s32[]{:S(2)}) async-start(), calls=%async_computation.2 | async-start | bytes 786432 | tf_op jit(solution)/shard_map/psum | solution.py:9
Sparse Core Ops, SparseCore 0:
  11.1 84.4 all-gather.1
  103.2 120.3 all-reduce.8
  259.9 156.8 all-reduce.4
  418.9 116.0 all-reduce.6
where the time goes:
time: 568 us; the launch traced here: 567 us
  waiting for transfers between devices  449 us (79%)
  other arithmetic  31.8 us (6%)
  blocking collectives  29.8 us (5%)
  local copies, waits for them, and re-layouts  24.8 us (4%)
  matrix products  16.9 us (3%)
  between operations  13.9 us (2%)
    psum x3, waiting for transfers between devices, from_root(): return lax.psum(kept, axis)  392 us
    all_gather x1, waiting for transfers between devices, shards(): features = lax.all_gather(embeddings, 'pcol', axis=3, tiled=True)  57 us
    psum x1, blocking collectives, from_root(): return lax.psum(kept, axis)  29.8 us
    another operation x3, other arithmetic, shards(): factor = jnp.linalg.cholesky(first_kernel)  12.4 us
    unnamed x7, local copies, waits for them, and re-layouts  12.1 us
  transfers between devices with their start and end apart: 4, of which 4 were waited for; matrix products, arithmetic and copies ran while one was open for 0% of the time, Pallas kernels for 0%

commit v1 on v0

--- a/solution.py
+++ b/solution.py
@@ -25,7 +25,9 @@
     col_count = lax.axis_size("pcol")
     row_index = lax.axis_index("prow")
     col_index = lax.axis_index("pcol")
-    features = lax.all_gather(embeddings, "pcol", axis=3, tiled=True)
+    features = jnp.concatenate(
+        lax.all_to_all(jnp.stack([embeddings] * lax.axis_size("pcol")), "pcol", 0, 0), axis=3
+    )
     row_tiles = features.shape[0]
     tile_size = features.shape[2]
     feat_width = features.shape[3]

time: 568 us -> 544 us (0.958)
  waiting for transfers between devices: 449 us -> 411 us
  starting transfers between devices: 0.34 us -> 14.1 us
  local copies, waits for them, and re-layouts: 24.8 us -> 32.6 us
    all_gather x1 -> x0, waiting for transfers between devices: 57 us -> none  [shards(): features = lax.all_gather(embeddings, 'pcol', axis=3, tiled=True)]
    all_to_all x0 -> x1, waiting for transfers between devices: none -> 28.3 us  [shards(): lax.all_to_all(jnp.stack([embeddings] * lax.axis_size('pcol')), 'pcol', 0...]
    all_to_all x0 -> x1, starting transfers between devices: none -> 13.7 us  [shards(): lax.all_to_all(jnp.stack([embeddings] * lax.axis_size('pcol')), 'pcol', 0...]
    psum x3, waiting for transfers between devices: 392 us -> 383 us  [from_root(): return lax.psum(kept, axis)]
    reshape x0 -> x1, local copies, waits for them, and re-layouts: none -> 5.76 us  [shards(): jnp.concatenate(lax.all_to_all(jnp.stack([embeddings] * lax.axis_size('pc...]
    unnamed x7 -> x9, local copies, waits for them, and re-layouts: 12.1 us -> 12.8 us
  transfers between devices with their start and end apart: 4 -> 4, of which waited for: 4 -> 4; matrix products, arithmetic and copies ran while one was open for 0% -> 1% of each run, Pallas kernels for 0% -> 0%
where the time goes in v1:
time: 544 us
  waiting for transfers between devices  411 us (76%)
  local copies, waits for them, and re-layouts  32.6 us (6%)
  other arithmetic  29.8 us (5%)
  blocking collectives  25.4 us (5%)
  matrix products  16.4 us (3%)
  starting transfers between devices  14.1 us (3%)
  between operations  13.9 us (3%)
    psum x3, waiting for transfers between devices, from_root(): return lax.psum(kept, axis)  383 us
    all_to_all x1, waiting for transfers between devices, shards(): lax.all_to_all(jnp.stack([embeddings] * lax.axis_size('pcol')), 'pcol', 0...  28.3 us
    psum x1, blocking collectives, from_root(): return lax.psum(kept, axis)  25.4 us
    all_to_all x1, starting transfers between devices, shards(): lax.all_to_all(jnp.stack([embeddings] * lax.axis_size('pcol')), 'pcol', 0...  13.7 us
    unnamed x9, local copies, waits for them, and re-layouts  12.8 us
    another operation x3, other arithmetic, shards(): factor = jnp.linalg.cholesky(first_kernel)  12.4 us
  transfers between devices with their start and end apart: 4, of which 4 were waited for; matrix products, arithmetic and copies ran while one was open for 1% of the time, Pallas kernels for 0%

profile of v1, /device:TPU:1, one launch (start us, length us, event | category | flops | bytes accessed | tf_op | source)
XLA Modules:
  0.0 543.5 jit_solution(4351422885183234728)
XLA Ops:
  7.2 2.6 stack.2
  9.8 13.7 %all-to-all-start = ((bf16[32,12,1,128,24]{3,4,1,2,0:T(8,128)(2,1)}), bf16[32,12,1,128,24]{3,4,1,2,0:T(8,128)(2,1)S(1)}, u32[]{:S(2)}, u32[]{:S(2)}) async-start(bf16[32,12,1,128,24]{3,4,1,2,0:T(8,128)(2,1)} %stack.2), calls=%async_computation | async-start | bytes 4718592 | tf_op jit(solution)/shard_map/all_to_all | solution.py:29
  23.6 25.4 %psum.37 = bf16[128]{0:T(256)(128)(2,1)S(1)} all-reduce(bf16[128]{0:T(256)(128)(2,1)S(1)} %fusion.10), channel_id=1, replica_groups=mesh['prow'=16,'pcol'=32] {'prow'}, use_global_device_ids=true, to_apply=%region_5.6 | all-reduce | flops 128 | bytes 512 | tf_op jit(solution)/shard_map/psum | solution.py:9
  49.1 28.3 %all-to-all-done = bf16[32,12,1,128,24]{3,4,1,2,0:T(8,128)(2,1)S(1)} async-done(((bf16[32,12,1,128,24]{3,4,1,2,0:T(8,128)(2,1)}), bf16[32,12,1,128,24]{3,4,1,2,0:T(8,128)(2,1)S(1)}, u32[]{:S(2)}, u32[]{:S(2)}) %all-to-all-start) | async-done | bytes 2359328 | tf_op jit(solution)/shard_map/all_to_all | solution.py:29
  78.0 0.7 slice_select_fusion
  79.4 1.1 select_bitcast_fusion
  80.7 5.8 %copy.27 = bf16[12,1,128,32,24]{2,0,4,3,1:T(8,128)(2,1)} copy(bf16[12,1,128,32,24]{2,4,3,0,1:T(8,128)(2,1)} %bitcast.62) | data formatting | bytes 4718592 | tf_op jit(solution)/shard_map/reshape | solution.py:28
  86.9 111.3 %all-reduce.9.cloned.1.call-done = (bf16[6,128,768]{1,2,0:T(8,128)(2,1)}, bf16[128,768]{0,1:T(8,128)(2,1)}) async-done(((bf16[6,128,768]{1,2,0:T(8,128)(2,1)}, bf16[128,768]{0,1:T(8,128)(2,1)}), (bf16[6,128,768]{1,2,0:T(8,128)(2,1)}, bf16[128,768]{0,1:T(8,128)(2,1)})) %all-reduce.9.cloned.1.call-update) | async-done | bytes 1376272 | tf_op jit(solution)/shard_map/psum | solution.py:9
  198.2 1.5 multiply_reduce_fusion.1
  199.7 2.6 copy.26
  202.3 1.0 multiply_reduce_fusion.2
  203.3 1.3 broadcast_add_fusion
  204.9 11.7 %cholesky.16 = f32[128,128]{1,0:T(8,128)S(1)} custom-call(f32[128,128]{1,0:T(8,128)S(1)} %add_multiply_fusion), custom_call_target="Cholesky" | custom-call | tf_op jit(solution)/shard_map/jit(cholesky)/cholesky | solution.py:67
  217.9 9.8 %custom-call.6 = f32[1,128,128]{1,2,0:T(8,128)S(1)} custom-call(f32[1,128,128]{2,1,0:T(8,128)S(1)} %fusion.7), custom_call_target="InvertDiagBlocksLowerTriangular" | custom-call | tf_op jit(solution)/shard_map/triangular_solve | solution.py:68
  227.8 4.0 fusion.3
  231.8 2.2 copy-done.1
  234.0 2.3 convolution_select_fusion
  236.6 156.7 %all-reduce.5.cloned.1.call-done = f32[1536,128]{1,0:T(8,128)} async-done(((f32[1536,128]{1,0:T(8,128)}), f32[1536,128]{1,0:T(8,128)}) %all-reduce.5.cloned.1.call-update) | async-done | bytes 786448 | tf_op jit(solution)/shard_map/psum | solution.py:9
  393.3 1.8 dynamic-slice_select_fusion
  395.1 1.4 constant_dynamic-slice_fusion
  396.5 115.1 %all-reduce.7.cloned.1.call-done = f32[768,128]{1,0:T(8,128)} async-done(((f32[768,128]{1,0:T(8,128)}), f32[768,128]{1,0:T(8,128)}) %all-reduce.7.cloned.1.call-update) | async-done | bytes 393232 | tf_op jit(solution)/shard_map/psum | solution.py:9
  511.7 8.7 %convolution_subtract_fusion = f32[1536,768]{0,1:T(8,128)} fusion(f32[1536,768]{0,1:T(8,128)} %copy-done.1, f32[1536,128]{1,0:T(8,128)} %all-reduce.5.cloned.1.call-done, f32[768,128]{1,0:T(8,128)} %all-reduce.7.cloned.1.call-done), kind=kOutput, calls=%fused_computation.6 | convolution fusion | flops 1813118976 | bytes 10616832 | tf_op jit(solution)/shard_map/dot_general | solution.py:75
  520.4 6.7 %reshape.118 = f32[12,1,128,6,1,128]{2,0,5,3,4,1:T(8,128)} reshape(f32[1536,768]{0,1:T(8,128)} %convolution_subtract_fusion) | data formatting | bytes 9437184 | tf_op jit(solution)/shard_map/reshape | solution.py:82
  527.1 9.9 %copy.33 = f32[12,1,128,6,1,128]{5,4,3,2,1,0:T(1,128)} copy(f32[12,1,128,6,1,128]{2,0,5,3,4,1:T(8,128)} %reshape.118) | data formatting | bytes 9437184
  (28 shorter events, 3.9 us)
Async XLA Ops:
  7.2 16.4 %copy-start.3 = (bf16[12,1,128]{2,0,1:T(8,128)(2,1)S(1)}, bf16[12,1,128]{2,0,1:T(8,128)(2,1)}, u32[]{:S(2)}) copy-start(bf16[12,1,128]{2,0,1:T(8,128)(2,1)} %param.3) | copy-start | bytes 9220
  9.8 67.6 %all-to-all-start = ((bf16[32,12,1,128,24]{3,4,1,2,0:T(8,128)(2,1)}), bf16[32,12,1,128,24]{3,4,1,2,0:T(8,128)(2,1)S(1)}, u32[]{:S(2)}, u32[]{:S(2)}) async-start(bf16[32,12,1,128,24]{3,4,1,2,0:T(8,128)(2,1)} %stack.2), calls=%async_computation | async-start | bytes 4718592 | tf_op jit(solution)/shard_map/all_to_all | solution.py:29
  23.5 174.7 %all-reduce.9.cloned.1.call-start = ((), (), s32[]{:S(2)}) async-start(), calls=%async_computation.3 | async-start | bytes 2752512 | tf_op jit(solution)/shard_map/psum | solution.py:9
  77.9 1.5 copy-start
  80.5 312.8 %all-reduce.5.cloned.1.call-start = ((), (), s32[]{:S(2)}) async-start(), calls=%async_computation.1 | async-start | bytes 1572864 | tf_op jit(solution)/shard_map/psum | solution.py:9
  86.9 140.9 %copy-start.2 = (bf16[12,1,128,32,24]{2,0,4,3,1:T(8,128)(2,1)S(1)}, bf16[12,1,128,32,24]{2,0,4,3,1:T(8,128)(2,1)}, u32[]{:S(2)}) copy-start(bf16[12,1,128,32,24]{2,0,4,3,1:T(8,128)(2,1)} %copy.27) | copy-start | bytes 7077892
  231.8 2.2 copy-start.1
  236.3 275.3 %all-reduce.7.cloned.1.call-start = ((), (), s32[]{:S(2)}) async-start(), calls=%async_computation.2 | async-start | bytes 786432 | tf_op jit(solution)/shard_map/psum | solution.py:9
Sparse Core Ops, SparseCore 0:
  80.6 117.5 all-reduce.8
  236.5 156.7 all-reduce.4
  395.6 116.0 all-reduce.6

commit v2 on v0

--- a/solution.py
+++ b/solution.py
@@ -6,7 +6,7 @@
 
 def from_root(value, axis, source):
     kept = jnp.where(lax.axis_index(axis) == source, value, 0).astype(value.dtype)
-    return lax.psum(kept, axis)
+    return jnp.sum(lax.all_gather(kept, axis), axis=0)
 
 
 def squares(values):

time: 568 us -> 549 us (0.967)
  waiting for transfers between devices: 449 us -> 423 us
  other arithmetic: 31.8 us -> 52.3 us
  blocking collectives: 29.8 us -> 20.4 us
    psum x3 -> x0, waiting for transfers between devices: 392 us -> none  [from_root(): return lax.psum(kept, axis)]
    all_gather x0 -> x4, waiting for transfers between devices: none -> 334 us  [from_root(): return jnp.sum(lax.all_gather(kept, axis), axis=0)]
    all_gather x1, waiting for transfers between devices: 57 us -> 87.5 us  [shards(): features = lax.all_gather(embeddings, 'pcol', axis=3, tiled=True)]
    psum x1 -> x0, blocking collectives: 29.8 us -> none  [from_root(): return lax.psum(kept, axis)]
    reduce_sum x0 -> x5, other arithmetic: none -> 25.2 us  [from_root(): return jnp.sum(lax.all_gather(kept, axis), axis=0)]
    all_gather x0 -> x1, blocking collectives: none -> 20.4 us  [from_root(): return jnp.sum(lax.all_gather(kept, axis), axis=0)]
    unnamed x7 -> x10, local copies, waits for them, and re-layouts: 12.1 us -> 13.7 us
  transfers between devices with their start and end apart: 4 -> 5, of which waited for: 4 -> 5; matrix products, arithmetic and copies ran while one was open for 0% -> 6% of each run, Pallas kernels for 0% -> 0%
where the time goes in v2:
time: 549 us
  waiting for transfers between devices  423 us (77%)
  other arithmetic  52.3 us (10%)
  local copies, waits for them, and re-layouts  26.8 us (5%)
  blocking collectives  20.4 us (4%)
  between operations  14 us (3%)
  matrix products  12.3 us (2%)
    all_gather x4, waiting for transfers between devices, from_root(): return jnp.sum(lax.all_gather(kept, axis), axis=0)  334 us
    all_gather x1, waiting for transfers between devices, shards(): features = lax.all_gather(embeddings, 'pcol', axis=3, tiled=True)  87.5 us
    reduce_sum x5, other arithmetic, from_root(): return jnp.sum(lax.all_gather(kept, axis), axis=0)  25.2 us
    all_gather x1, blocking collectives, from_root(): return jnp.sum(lax.all_gather(kept, axis), axis=0)  20.4 us
    unnamed x10, local copies, waits for them, and re-layouts  13.7 us
    another operation x3, other arithmetic, shards(): factor = jnp.linalg.cholesky(first_kernel)  12.4 us
  transfers between devices with their start and end apart: 5, of which 5 were waited for; matrix products, arithmetic and copies ran while one was open for 6% of the time, Pallas kernels for 0%

profile of v2, /device:TPU:1, one launch (start us, length us, event | category | flops | bytes accessed | tf_op | source)
XLA Modules:
  0.0 548.7 jit_solution(2578137399290707713)
XLA Ops:
  8.0 87.5 %all-gather.11.cloned.1.call-done = bf16[12,1,128,768]{2,3,1,0:T(8,128)(2,1)} async-done(((bf16[12,1,128,24]{2,3,1,0:T(8,128)(2,1)}), bf16[12,1,128,768]{2,3,1,0:T(8,128)(2,1)}) %all-gather.11.cloned.1.call-update) | async-done | bytes 2359312 | tf_op jit(solution)/shard_map/all_gather | solution.py:28
  95.4 1.1 slice_select_fusion
  96.5 0.8 copy.25
  97.5 2.4 constant_dynamic-slice_fusion.1
  99.8 1.6 copy.35
  101.4 1.2 broadcast_select_fusion
  102.7 20.4 %all-gather.2 = bf16[16,1,128]{2,1,0:T(2,128)(2,1)S(1)} all-gather(bf16[1,1,128]{2,1,0:T(2,128)(2,1)S(1)} %broadcast_select_fusion.1), channel_id=4, replica_groups=mesh['prow'=16,'pcol'=32] {'prow'}, dimensions={0}, use_global_device_ids=true | all-gather | bytes 4352 | tf_op jit(solution)/shard_map/all_gather | solution.py:9
  123.3 2.4 copy.24
  126.2 17.8 %all-gather.15.cloned.1.call-done = bf16[16,1,128,768]{3,2,1,0:T(8,128)(2,1)} async-done(((bf16[1,1,128,768]{3,2,1,0:T(8,128)(2,1)}), bf16[16,1,128,768]{3,2,1,0:T(8,128)(2,1)}) %all-gather.15.cloned.1.call-update) | async-done | bytes 3145744 | tf_op jit(solution)/shard_map/all_gather | solution.py:9
  143.9 2.3 reduce_sum.84
  146.9 11.7 %cholesky.16 = f32[128,128]{1,0:T(8,128)S(1)} custom-call(f32[128,128]{1,0:T(8,128)S(1)} %add_multiply_fusion), custom_call_target="Cholesky" | custom-call | tf_op jit(solution)/shard_map/jit(cholesky)/cholesky | solution.py:65
  159.9 9.8 %custom-call.6 = f32[1,128,128]{1,2,0:T(8,128)S(1)} custom-call(f32[1,128,128]{2,1,0:T(8,128)S(1)} %fusion.5), custom_call_target="InvertDiagBlocksLowerTriangular" | custom-call | tf_op jit(solution)/shard_map/triangular_solve | solution.py:66
  169.8 82.9 %all-gather.13.cloned.1.call-done = bf16[96,1,128,768]{3,2,1,0:T(8,128)(2,1)} async-done(((bf16[6,1,128,768]{3,2,1,0:T(8,128)(2,1)}), bf16[96,1,128,768]{3,2,1,0:T(8,128)(2,1)}) %all-gather.13.cloned.1.call-update) | async-done | bytes 18874384 | tf_op jit(solution)/shard_map/all_gather | solution.py:9
  252.7 10.5 %bitcast_reduce_fusion = bf16[6,128,768]{2,1,0:T(8,128)(2,1)S(1)} fusion(bf16[16,6,128,768]{3,2,1,0:T(8,128)(2,1)} %bitcast.52), kind=kLoop, calls=%fused_computation | loop fusion | flops 8847360 | bytes 20054016 | tf_op jit(solution)/shard_map/reduce_sum | solution.py:9
  263.5 2.6 fusion.3
  266.1 2.2 copy-done.1
  268.3 2.3 convolution_select_fusion
  270.7 188.4 %all-gather.17.cloned.1.call-done = f32[49152,128]{1,0:T(8,128)} async-done(((f32[1536,128]{1,0:T(8,128)}), f32[49152,128]{1,0:T(8,128)}) %all-gather.17.cloned.1.call-update) | async-done | bytes 25165840 | tf_op jit(solution)/shard_map/all_gather | solution.py:9
  459.1 9.2 %reduce_sum.87 = f32[1536,128]{1,0:T(8,128)S(1)} reduce(f32[32,1536,128]{2,1,0:T(8,128)} %bitcast.51, f32[]{:T(128)} %constant.92.clone.1), dimensions={0}, to_apply=%region_8.9 | reduce | flops 6094848 | bytes 25952260 | tf_op jit(solution)/shard_map/reduce_sum | solution.py:9
  469.8 45.4 %all-gather.19.cloned.1.call-done = f32[96,1,128,128]{3,2,1,0:T(8,128)} async-done(((f32[6,1,128,128]{3,2,1,0:T(8,128)}), f32[96,1,128,128]{3,2,1,0:T(8,128)}) %all-gather.19.cloned.1.call-update) | async-done | bytes 6291472 | tf_op jit(solution)/shard_map/all_gather | solution.py:9
  515.2 3.2 bitcast_reduce_fusion.1
  518.4 7.2 %convolution_subtract_fusion = f32[1536,768]{0,1:T(8,128)} fusion(f32[1536,768]{0,1:T(8,128)} %copy-done.1, f32[1536,128]{1,0:T(8,128)S(1)} %reduce_sum.87, f32[768,128]{1,0:T(8,128)S(1)} %bitcast.59), kind=kOutput, calls=%fused_computation.8 | convolution fusion | flops 1813118976 | bytes 10616832 | tf_op jit(solution)/shard_map/dot_general | solution.py:73
  525.5 6.7 %reshape.162 = f32[12,1,128,6,1,128]{2,0,5,3,4,1:T(8,128)} reshape(f32[1536,768]{0,1:T(8,128)} %convolution_subtract_fusion) | data formatting | bytes 9437184 | tf_op jit(solution)/shard_map/reshape | solution.py:80
  532.2 9.9 %copy.31 = f32[12,1,128,6,1,128]{5,4,3,2,1,0:T(1,128)} copy(f32[12,1,128,6,1,128]{2,0,5,3,4,1:T(8,128)} %reshape.162) | data formatting | bytes 9437184
  (37 shorter events, 5.3 us)
Async XLA Ops:
  7.2 95.5 %copy-start.3 = (bf16[12,1,128]{2,0,1:T(8,128)(2,1)S(1)}, bf16[12,1,128]{2,0,1:T(8,128)(2,1)}, u32[]{:S(2)}) copy-start(bf16[12,1,128]{2,0,1:T(8,128)(2,1)} %param.3) | copy-start | bytes 9220
  7.2 88.3 %all-gather.11.cloned.1.call-start = ((), (), s32[]{:S(2)}) async-start(), calls=%async_computation | async-start | bytes 2433024 | tf_op jit(solution)/shard_map/all_gather | solution.py:28
  7.9 136.0 %all-gather.15.cloned.1.call-start = ((), (), s32[]{:S(2)}) async-start(), calls=%async_computation.2 | async-start | bytes 3342336 | tf_op jit(solution)/shard_map/all_gather | solution.py:9
  95.4 27.8 %copy-start = (bf16[12,1,128,768]{2,3,1,0:T(8,128)(2,1)S(1)}, bf16[12,1,128,768]{2,3,1,0:T(8,128)(2,1)}, u32[]{:S(2)}) copy-start(bf16[12,1,128,768]{2,3,1,0:T(8,128)(2,1)} %all-gather.11.cloned.1.call-done) | copy-start | bytes 7077892
  97.4 155.3 %all-gather.13.cloned.1.call-start = ((), (), s32[]{:S(2)}) async-start(), calls=%async_computation.1 | async-start | bytes 20054016 | tf_op jit(solution)/shard_map/all_gather | solution.py:9
  102.6 356.5 %all-gather.17.cloned.1.call-start = ((), (), s32[]{:S(2)}) async-start(), calls=%async_computation.3 | async-start | bytes 25952256 | tf_op jit(solution)/shard_map/all_gather | solution.py:9
  252.7 10.8 %copy-start.2 = (bf16[12,1,128,768]{3,2,0,1:T(8,128)(2,1)S(1)}, bf16[12,1,128,768]{3,2,0,1:T(8,128)(2,1)}, u32[]{:S(2)}) copy-start(bf16[12,1,128,768]{3,2,0,1:T(8,128)(2,1)} %copy.24) | copy-start | bytes 7077892
  266.1 2.2 copy-start.1
  270.7 244.5 %all-gather.19.cloned.1.call-start = ((), (), s32[]{:S(2)}) async-start(), calls=%async_computation.4 | async-start | bytes 6684672 | tf_op jit(solution)/shard_map/all_gather | solution.py:9
Sparse Core Ops, SparseCore 0:
  11.1 84.2 all-gather.10
  97.6 46.3 all-gather.14
  146.0 106.6 all-gather.12
  270.8 188.2 all-gather.16
  469.3 45.8 all-gather.18
